TPU v7x, 32 devices: a whole 2x2x4 slice. The times are simulated.
32 devices in a mesh: row: 4 (over z), col: 4 (over x, core), layer: 2 (over y).
Axes of the slice: x: 2, y: 2, z: 4, core: 2. Of those that a mesh axis runs over, the one named last changes fastest.
Arguments:
- intersection: bfloat16 [2048, 2, 1024], P('row', 'layer', 'col'), may hold values from -6 to 6
- density: bfloat16 [2, 1024, 2, 1024], P('layer', 'row', None, 'col'), may hold values from -0.125 to 0.125
- hamiltonian: bfloat16 [2, 1024, 2, 1024], P('layer', 'row', None, 'col'), may hold values from -0.125 to 0.125
- intersection_pattern: int32 [16, 2, 8], P('row', 'layer', 'col'), may hold values 0 or 1
- density_pattern: int32 [2, 8, 2, 8], P('layer', 'row', None, 'col'), may hold values 0 or 1
- hamiltonian_pattern: int32 [2, 8, 2, 8], P('layer', 'row', None, 'col'), may hold values 0 or 1
- product_filter: int32 [16, 2, 8], P('row', 'layer', 'col'), may hold values 0 or 1
Outputs:
- gradient_term: bfloat16 [2048, 2, 1024], P('row', 'layer', 'col')
All inputs are finite; a program needn't handle non-finite values. No bound on the sum of `intersection_pattern` or of `density_pattern` or of `hamiltonian_pattern` or of `product_filter` on one device may be relied on, other than what follows from the above.
Results may differ from a plain program's by a relative error of at most 0.005.
Values may be sent and summed in bfloat16 or wider, within the bound.
No kernel may reach another device: no remote copies, remote signals or barrier semaphores. Data moves between devices by JAX's collectives and lax.ppermute only.
A program may use at most 64 MiB of HBM per device.

v0:
```python
import jax
import jax.numpy as jnp
from jax import lax
from jax.sharding import PartitionSpec as P


def mask_left(block_tile, pattern):
    row_count, _, col_count = block_tile.shape
    row_blocks = pattern.shape[0]
    col_blocks = pattern.shape[2]
    blocks = block_tile.reshape(
        row_blocks, row_count // row_blocks, col_blocks, col_count // col_blocks
    )
    blocks = blocks * pattern.reshape(row_blocks, 1, col_blocks, 1).astype(jnp.bfloat16)
    return blocks.reshape(row_count, col_count)


def mask_right(block_tile, pattern):
    _, row_count, layers, col_count = block_tile.shape
    row_blocks = pattern.shape[1]
    col_blocks = pattern.shape[3]
    blocks = block_tile.reshape(
        row_blocks, row_count // row_blocks, layers, col_blocks, col_count // col_blocks
    )
    blocks = blocks * pattern.reshape(row_blocks, 1, layers, col_blocks, 1).astype(jnp.bfloat16)
    return blocks.reshape(row_count, layers * col_count)


def multiply(left_tile, right_tile):
    whole_left = lax.all_gather(left_tile, "col", axis=1, tiled=True)
    row_count = whole_left.shape[0]
    layers = lax.axis_size("layer")
    column_span = right_tile.shape[1] // layers
    partial_value = jnp.dot(
        whole_left,
        lax.all_gather(right_tile, "row", axis=0, tiled=True),
        preferred_element_type=jnp.float32,
    )
    return lax.psum_scatter(
        partial_value.reshape(row_count, layers, column_span),
        "layer",
        scatter_dimension=1,
        tiled=True,
    )


def local(
    intersection,
    density,
    hamiltonian,
    intersection_pattern,
    density_pattern,
    hamiltonian_pattern,
    product_filter,
):
    left_factor = mask_left(intersection, intersection_pattern)
    right_factor = mask_right(density, density_pattern)
    raw_product = multiply(left_factor, right_factor)
    filtered = mask_left(raw_product.astype(jnp.bfloat16), product_filter)
    masked_ham = mask_right(hamiltonian, hamiltonian_pattern)
    return multiply(filtered, masked_ham).astype(jnp.bfloat16)


def solution(mesh):
    placed = (
        P("row", "layer", "col"),
        P("layer", "row", None, "col"),
        P("layer", "row", None, "col"),
        P("row", "layer", "col"),
        P("layer", "row", None, "col"),
        P("layer", "row", None, "col"),
        P("row", "layer", "col"),
    )
    return jax.shard_map(
        local, mesh=mesh, in_specs=placed, out_specs=P("row", "layer", "col"), check_vma=False
    )
```

profile of v0, /device:TPU:0, one launch (start us, length us, event | category | flops | bytes accessed | tf_op | source)
XLA Modules:
  0.0 161.6 jit_solution(11556054652740069047)
XLA Ops:
  6.5 0.7 convert_bitcast_fusion.1
  7.2 0.2 mul.47
  7.6 0.8 copy-done.1
  8.4 0.8 mul.49
  9.4 0.2 mul.44
  9.6 0.5 copy-done
  10.2 0.7 bitcast_multiply_fusion.1
  11.0 29.0 %all-gather.7.cloned.1.call-done = bf16[1024,512]{1,0:T(8,128)(2,1)} async-done(((bf16[256,512]{1,0:T(8,128)(2,1)}), bf16[1024,512]{1,0:T(8,128)(2,1)}) %all-gather.7.cloned.1.call-update) | async-done | bytes 1048592 | tf_op jit(solution)/shard_map/all_gather | solution.py:36
  40.0 17.9 %all-gather.5.cloned.1.call-done = bf16[512,1024]{1,0:T(8,128)(2,1)} async-done(((bf16[512,256]{1,0:T(8,128)(2,1)}), bf16[512,1024]{1,0:T(8,128)(2,1)}) %all-gather.5.cloned.1.call-update) | async-done | bytes 1048592 | tf_op jit(solution)/shard_map/all_gather | solution.py:30
  57.9 3.3 %fusion = f32[512,512]{0,1:T(8,128)} fusion(bf16[512,1024]{1,0:T(8,128)(2,1)} %all-gather.5.cloned.1.call-done, bf16[1024,512]{1,0:T(8,128)(2,1)} %all-gather.7.cloned.1.call-done), kind=kOutput, calls=%fused_computation.6 | convolution fusion | flops 536870912 | bytes 3145728 | tf_op jit(solution)/shard_map/dot_general | solution.py:34
  61.3 0.6 copy-done.3
  61.9 0.2 mul.53
  62.2 0.8 copy-done.2
  63.1 0.8 mul.55
  64.0 0.6 copy-done.5
  64.6 17.1 %reduce-scatter.3.cloned.1.call-done = f32[512,1,256]{0,2,1:T(8,128)} async-done(((f32[512,2,256]{0,2,1:T(8,128)}), f32[512,1,256]{0,2,1:T(8,128)}) %reduce-scatter.3.cloned.1.call-update) | async-done | bytes 524304 | tf_op jit(solution)/shard_map/reduce_scatter | solution.py:39
  81.7 0.1 mul.50
  81.9 1.8 %bitcast_multiply_fusion = bf16[512,256]{0,1:T(8,128)(2,1)} fusion(bf16[32,8,4,128]{3,2,1,0:T(4,128)(2,1)S(1)} %bitcast.39, f32[512,1,256]{0,2,1:T(8,128)} %reduce-scatter.3.cloned.1.call-done), kind=kLoop, calls=%fused_computation | loop fusion | flops 262144 | bytes 1048576 | tf_op jit(solution)/shard_map/mul | solution.py:14
  83.7 27.4 %all-gather.11.cloned.1.call-done = bf16[1024,512]{1,0:T(8,128)(2,1)} async-done(((bf16[256,512]{1,0:T(8,128)(2,1)}), bf16[1024,512]{1,0:T(8,128)(2,1)}) %all-gather.11.cloned.1.call-update) | async-done | bytes 1048592 | tf_op jit(solution)/shard_map/all_gather | solution.py:36
  111.2 17.7 %all-gather.9.cloned.1.call-done = bf16[512,1024]{0,1:T(8,128)(2,1)} async-done(((bf16[512,256]{0,1:T(8,128)(2,1)}), bf16[512,1024]{0,1:T(8,128)(2,1)}) %all-gather.9.cloned.1.call-update) | async-done | bytes 1048592 | tf_op jit(solution)/shard_map/all_gather | solution.py:30
  128.9 2.3 %fusion.1 = f32[512,512]{0,1:T(8,128)S(1)} fusion(bf16[512,1024]{0,1:T(8,128)(2,1)} %all-gather.9.cloned.1.call-done, bf16[1024,512]{1,0:T(8,128)(2,1)} %all-gather.11.cloned.1.call-done), kind=kOutput, calls=%fused_computation.7 | convolution fusion | flops 536870912 | bytes 3145728 | tf_op jit(solution)/shard_map/dot_general | solution.py:34
  131.2 1.3 copy.9
  132.5 20.5 %reduce-scatter.5.cloned.1.call-done = f32[512,1,256]{2,0,1:T(8,128)} async-done(((f32[512,2,256]{2,0,1:T(8,128)}), f32[512,1,256]{2,0,1:T(8,128)}) %reduce-scatter.5.cloned.1.call-update) | async-done | bytes 524304 | tf_op jit(solution)/shard_map/reduce_scatter | solution.py:39
  153.0 1.8 %convert_element_type.59 = bf16[512,1,256]{2,0,1:T(8,128)(2,1)} convert(f32[512,1,256]{2,0,1:T(8,128)} %reduce-scatter.5.cloned.1.call-done) | non-fusion elementwise | flops 131072 | bytes 786432 | tf_op jit(solution)/shard_map/convert_element_type | solution.py:61
  (27 shorter events, 0.7 us)
Async XLA Ops:
  6.5 33.5 %all-gather.7.cloned.1.call-start = ((), (), s32[]{:S(2)}) async-start(), calls=%async_computation.3 | async-start | bytes 1310720 | tf_op jit(solution)/shard_map/all_gather | solution.py:36
  7.4 1.0 copy-start.1
  8.4 0.9 copy-start.4
  9.2 0.9 copy-start
  9.2 48.7 %all-gather.5.cloned.1.call-start = ((), (), s32[]{:S(2)}) async-start(), calls=%async_computation.2 | async-start | bytes 1310720 | tf_op jit(solution)/shard_map/all_gather | solution.py:30
  10.9 70.8 %reduce-scatter.3.cloned.1.call-start = ((), (), s32[]{:S(2)}) async-start(), calls=%async_computation.4 | async-start | bytes 1572864 | tf_op jit(solution)/shard_map/reduce_scatter | solution.py:39
  61.2 0.7 copy-start.3
  61.2 49.9 %all-gather.11.cloned.1.call-start = ((), (), s32[]{:S(2)}) async-start(), calls=%async_computation.6 | async-start | bytes 1310720 | tf_op jit(solution)/shard_map/all_gather | solution.py:36
  62.1 1.0 copy-start.2
  63.9 0.7 copy-start.5
  63.9 65.0 %all-gather.9.cloned.1.call-start = ((), (), s32[]{:S(2)}) async-start(), calls=%async_computation.5 | async-start | bytes 1310720 | tf_op jit(solution)/shard_map/all_gather | solution.py:30
  83.7 69.3 %reduce-scatter.5.cloned.1.call-start = ((), (), s32[]{:S(2)}) async-start(), calls=%async_computation.7 | async-start | bytes 1572864 | tf_op jit(solution)/shard_map/reduce_scatter | solution.py:39
Sparse Core Ops, SparseCore 0:
  9.4 30.6 all-gather.6
  41.6 16.3 all-gather.4
  61.4 20.3 reduce-scatter.2
  83.2 27.9 all-gather.10
  112.7 16.2 all-gather.8
  132.7 20.3 reduce-scatter.4
where the time goes:
time: 162 us
  waiting for transfers between devices  130 us (80%)
  between operations  13.6 us (8%)
  other arithmetic  6.58 us (4%)
  local copies, waits for them, and re-layouts  5.88 us (4%)
  matrix products  5.57 us (3%)
    all_gather x2, waiting for transfers between devices, multiply(): lax.all_gather(right_tile, 'row', axis=0, tiled=True)  56.5 us
    reduce_scatter x2, waiting for transfers between devices, multiply(): lax.psum_scatter(partial_value.reshape(row_count, layers, column_span), '...  37.6 us
    all_gather x2, waiting for transfers between devices, multiply(): whole_left = lax.all_gather(left_tile, 'col', axis=1, tiled=True)  35.6 us
    dot_general x2, matrix products, multiply(): jnp.dot(whole_left, lax.all_gather(right_tile, 'row', axis=0, tiled=True)...  5.57 us
    unnamed x14, local copies, waits for them, and re-layouts  3.49 us
  transfers between devices with their start and end apart: 6, of which 6 were waited for; matrix products, arithmetic and copies ran while one was open for 3% of the time, Pallas kernels for 0%

commit v1 on v0

--- a/solution.py
+++ b/solution.py
@@ -2,6 +2,18 @@
 import jax.numpy as jnp
 from jax import lax
 from jax.sharding import PartitionSpec as P
+
+
+def collect(x, axis, dim):
+    ways, here = (lax.axis_size(axis), lax.axis_index(axis))
+    grown, reach = (x, 1)
+    while reach < ways:
+        theirs = lax.ppermute(grown, axis, [(d, d ^ reach) for d in range(ways)])
+        mine_first = jnp.concatenate([grown, theirs], axis=dim)
+        theirs_first = jnp.concatenate([theirs, grown], axis=dim)
+        grown = jnp.where(here & reach == 0, mine_first, theirs_first)
+        reach = 2 * reach
+    return grown
 
 
 def mask_left(block_tile, pattern):
@@ -27,7 +39,7 @@
 
 
 def multiply(left_tile, right_tile):
-    whole_left = lax.all_gather(left_tile, "col", axis=1, tiled=True)
+    whole_left = collect(left_tile, "col", 1)
     row_count = whole_left.shape[0]
     layers = lax.axis_size("layer")
     column_span = right_tile.shape[1] // layers

time: 162 us -> 125 us (0.77)
  waiting for transfers between devices: 130 us -> 91.3 us
  starting transfers between devices: 0.21 us -> 5.18 us
    all_gather x2 -> x0, waiting for transfers between devices: 35.6 us -> none  [multiply(): whole_left = lax.all_gather(left_tile, 'col', axis=1, tiled=True)]
    all_gather x2, waiting for transfers between devices: 56.5 us -> 38.4 us  [multiply(): lax.all_gather(right_tile, 'row', axis=0, tiled=True)]
    ppermute x0 -> x4, waiting for transfers between devices: none -> 14.9 us  [collect(): theirs = lax.ppermute(grown, axis, [(d, d ^ reach) for d in range(ways)])]
    ppermute x0 -> x4, starting transfers between devices: none -> 5.06 us  [collect(): theirs = lax.ppermute(grown, axis, [(d, d ^ reach) for d in range(ways)])]
    unnamed x14 -> x12, local copies, waits for them, and re-layouts: 3.49 us -> 1.68 us
  transfers between devices with their start and end apart: 6 -> 8, of which waited for: 6 -> 7; matrix products, arithmetic and copies ran while one was open for 3% -> 3% of each run, Pallas kernels for 0% -> 0%
where the time goes in v1:
time: 125 us
  waiting for transfers between devices  91.3 us (73%)
  between operations  13.3 us (11%)
  local copies, waits for them, and re-layouts  5.58 us (4%)
  other arithmetic  5.39 us (4%)
  starting transfers between devices  5.18 us (4%)
  matrix products  3.97 us (3%)
    all_gather x2, waiting for transfers between devices, multiply(): lax.all_gather(right_tile, 'row', axis=0, tiled=True)  38.4 us
    reduce_scatter x2, waiting for transfers between devices, multiply(): lax.psum_scatter(partial_value.reshape(row_count, layers, column_span), '...  37.9 us
    ppermute x4, waiting for transfers between devices, collect(): theirs = lax.ppermute(grown, axis, [(d, d ^ reach) for d in range(ways)])  14.9 us
    ppermute x4, starting transfers between devices, collect(): theirs = lax.ppermute(grown, axis, [(d, d ^ reach) for d in range(ways)])  5.06 us
    dot_general x2, matrix products, multiply(): jnp.dot(whole_left, lax.all_gather(right_tile, 'row', axis=0, tiled=True)...  3.97 us
    reshape x2, local copies, waits for them, and re-layouts, multiply(): partial_value.reshape(row_count, layers, column_span)  2.65 us
  transfers between devices with their start and end apart: 8, of which 7 were waited for; matrix products, arithmetic and copies ran while one was open for 3% of the time, Pallas kernels for 0%

profile of v1, /device:TPU:0, one launch (start us, length us, event | category | flops | bytes accessed | tf_op | source)
XLA Modules:
  0.0 124.7 jit_solution(8520556855744008546)
XLA Ops:
  6.5 0.7 convert_bitcast_fusion.1
  7.2 0.2 mul.47
  7.6 1.0 copy.13
  8.6 0.8 mul.49
  9.6 0.2 mul.44
  9.8 0.5 collective-permute-start
  10.4 1.2 collective-permute-done
  11.6 2.9 %collective-permute-start.1 = (bf16[512,512]{1,0:T(8,128)(2,1)S(1)}, bf16[512,512]{1,0:T(8,128)(2,1)S(1)}, u32[]{:S(2)}, u32[]{:S(2)}) collective-permute-start(bf16[512,512]{1,0:T(8,128)(2,1)S(1)} %maximum_select_fusion.4), channel_id=1, source_target_pairs={{0,4},{2,6},{4,0},{6,2},{1,5},{3,7},{5,1},{7,3},{8,12},{10,14},{12... | collective-permute-start | bytes 1572872 | tf_op jit(solution)/shard_map/ppermute | solution.py:11
  14.6 12.2 %collective-permute-done.1 = bf16[512,512]{1,0:T(8,128)(2,1)S(1)} collective-permute-done((bf16[512,512]{1,0:T(8,128)(2,1)S(1)}, bf16[512,512]{1,0:T(8,128)(2,1)S(1)}, u32[]{:S(2)}, u32[]{:S(2)}) %collective-permute-start.1) | collective-permute-done | bytes 524320 | tf_op jit(solution)/shard_map/ppermute | solution.py:11
  26.8 13.4 %all-gather.3.cloned.1.call-done = bf16[1024,512]{1,0:T(8,128)(2,1)} async-done(((bf16[256,512]{1,0:T(8,128)(2,1)}), bf16[1024,512]{1,0:T(8,128)(2,1)}) %all-gather.3.cloned.1.call-update) | async-done | bytes 1048592 | tf_op jit(solution)/shard_map/all_gather | solution.py:48
  40.2 2.0 %fusion = f32[512,512]{0,1:T(8,128)S(1)} fusion(bf16[1024,512]{1,0:T(8,128)(2,1)} %all-gather.3.cloned.1.call-done, bf16[512,512]{1,0:T(8,128)(2,1)S(1)} %collective-permute-done.1, bf16[512,512]{1,0:T(8,128)(2,1)S(1)} %maximum_select_fusion.4, pred[]{:T(512)S(6)} %eq.8), kind=kOutput, calls=%fused_computation.1 | convolution fusion | flops 541589504 | bytes 3145729 | tf_op jit(solution)/shard_map/dot_general | solution.py:46
  42.2 1.3 %copy.9 = f32[512,2,256]{2,0,1:T(8,128)} copy(f32[512,2,256]{0,2,1:T(8,128)S(1)} %bitcast.34) | data formatting | bytes 2097152 | tf_op jit(solution)/shard_map/reshape | solution.py:52
  43.6 0.6 copy-done.2
  44.2 0.2 mul.53
  44.6 0.8 mul.55
  45.5 18.0 %reduce-scatter.3.cloned.1.call-done = f32[512,1,256]{2,0,1:T(8,128)} async-done(((f32[512,2,256]{2,0,1:T(8,128)}), f32[512,1,256]{2,0,1:T(8,128)}) %reduce-scatter.3.cloned.1.call-update) | async-done | bytes 524304 | tf_op jit(solution)/shard_map/reduce_scatter | solution.py:51
  63.7 1.1 bitcast_multiply_fusion
  64.9 1.5 %collective-permute-done.2 = bf16[512,256]{1,0:T(8,128)(2,1)S(1)} collective-permute-done((bf16[512,256]{1,0:T(8,128)(2,1)S(1)}, bf16[512,256]{1,0:T(8,128)(2,1)S(1)}, u32[]{:S(2)}, u32[]{:S(2)}) %collective-permute-start.2) | collective-permute-done | bytes 262176 | tf_op jit(solution)/shard_map/ppermute | solution.py:11
  66.5 1.5 %collective-permute-start.3 = (bf16[512,512]{1,0:T(8,128)(2,1)S(1)}, bf16[512,512]{1,0:T(8,128)(2,1)S(1)}, u32[]{:S(2)}, u32[]{:S(2)}) collective-permute-start(bf16[512,512]{1,0:T(8,128)(2,1)S(1)} %maximum_select_fusion.5), channel_id=1, source_target_pairs={{0,4},{2,6},{4,0},{6,2},{1,5},{3,7},{5,1},{7,3},{8,12},{10,14},{12... | collective-permute-start | bytes 1572872 | tf_op jit(solution)/shard_map/ppermute | solution.py:11
  68.1 25.0 %all-gather.5.cloned.1.call-done = bf16[1024,512]{1,0:T(8,128)(2,1)} async-done(((bf16[256,512]{1,0:T(8,128)(2,1)}), bf16[1024,512]{1,0:T(8,128)(2,1)}) %all-gather.5.cloned.1.call-update) | async-done | bytes 1048592 | tf_op jit(solution)/shard_map/all_gather | solution.py:48
  93.1 2.0 %fusion.6 = f32[512,512]{0,1:T(8,128)S(1)} fusion(bf16[1024,512]{1,0:T(8,128)(2,1)} %all-gather.5.cloned.1.call-done, bf16[512,512]{1,0:T(8,128)(2,1)S(1)} %collective-permute-done.3, bf16[512,512]{1,0:T(8,128)(2,1)S(1)} %maximum_select_fusion.5, pred[]{:T(512)S(6)} %eq.8), kind=kOutput, calls=%fused_computation.8 | convolution fusion | flops 541589504 | bytes 3145729 | tf_op jit(solution)/shard_map/dot_general | solution.py:46
  95.1 1.3 %copy.11 = f32[512,2,256]{2,0,1:T(8,128)} copy(f32[512,2,256]{0,2,1:T(8,128)S(1)} %bitcast.33) | data formatting | bytes 2097152 | tf_op jit(solution)/shard_map/reshape | solution.py:52
  96.5 19.9 %reduce-scatter.5.cloned.1.call-done = f32[512,1,256]{2,0,1:T(8,128)} async-done(((f32[512,2,256]{2,0,1:T(8,128)}), f32[512,1,256]{2,0,1:T(8,128)}) %reduce-scatter.5.cloned.1.call-update) | async-done | bytes 524304 | tf_op jit(solution)/shard_map/reduce_scatter | solution.py:51
  116.4 1.8 %convert_element_type.59 = bf16[512,1,256]{2,0,1:T(8,128)(2,1)} convert(f32[512,1,256]{2,0,1:T(8,128)} %reduce-scatter.5.cloned.1.call-done) | non-fusion elementwise | flops 131072 | bytes 786432 | tf_op jit(solution)/shard_map/convert_element_type | solution.py:73
  (31 shorter events, 1.2 us)
Async XLA Ops:
  6.5 33.6 %all-gather.3.cloned.1.call-start = ((), (), s32[]{:S(2)}) async-start(), calls=%async_computation.2 | async-start | bytes 1310720 | tf_op jit(solution)/shard_map/all_gather | solution.py:48
  7.4 2.0 %copy-start.3 = (s32[4,1,2]{0,2,1:T(2,128)S(1)}, s32[4,1,2]{0,2,1:T(2,128)}, u32[]{:S(2)}) copy-start(s32[4,1,2]{0,2,1:T(2,128)} %param.10) | copy-start | bytes 100
  7.6 2.2 %copy-start = (bf16[512,1,256]{2,0,1:T(8,128)(2,1)S(1)}, bf16[512,1,256]{2,0,1:T(8,128)(2,1)}, u32[]{:S(2)}) copy-start(bf16[512,1,256]{2,0,1:T(8,128)(2,1)} %param.7) | copy-start | bytes 786436
  9.4 54.1 %reduce-scatter.3.cloned.1.call-start = ((), (), s32[]{:S(2)}) async-start(), calls=%async_computation.3 | async-start | bytes 1572864 | tf_op jit(solution)/shard_map/reduce_scatter | solution.py:51
  9.8 1.7 %collective-permute-start = (bf16[512,256]{1,0:T(8,128)(2,1)S(1)}, bf16[512,256]{1,0:T(8,128)(2,1)S(1)}, u32[]{:S(2)}, u32[]{:S(2)}) collective-permute-start(bf16[512,256]{1,0:T(8,128)(2,1)S(1)} %bitcast_multiply_fusion.1), channel_id=1, source_target_pairs={{0,2},{2,0},{4,6},{6,4},{1,3},{3,1},{5,7},{7,5},{8,10},{10,8},{12,... | collective-permute-start | bytes 786440 | tf_op jit(solution)/shard_map/ppermute | solution.py:11
  11.6 15.2 %collective-permute-start.1 = (bf16[512,512]{1,0:T(8,128)(2,1)S(1)}, bf16[512,512]{1,0:T(8,128)(2,1)S(1)}, u32[]{:S(2)}, u32[]{:S(2)}) collective-permute-start(bf16[512,512]{1,0:T(8,128)(2,1)S(1)} %maximum_select_fusion.4), channel_id=1, source_target_pairs={{0,4},{2,6},{4,0},{6,2},{1,5},{3,7},{5,1},{7,3},{8,12},{10,14},{12... | collective-permute-start | bytes 1572872 | tf_op jit(solution)/shard_map/ppermute | solution.py:11
  43.5 0.7 copy-start.2
  43.5 1.0 copy-start.1
  43.5 49.6 %all-gather.5.cloned.1.call-start = ((), (), s32[]{:S(2)}) async-start(), calls=%async_computation.4 | async-start | bytes 1310720 | tf_op jit(solution)/shard_map/all_gather | solution.py:48
  44.4 1.0 copy-start.4
  45.4 71.0 %reduce-scatter.5.cloned.1.call-start = ((), (), s32[]{:S(2)}) async-start(), calls=%async_computation.5 | async-start | bytes 1572864 | tf_op jit(solution)/shard_map/reduce_scatter | solution.py:51
  64.8 1.6 %collective-permute-start.2 = (bf16[512,256]{1,0:T(8,128)(2,1)S(1)}, bf16[512,256]{1,0:T(8,128)(2,1)S(1)}, u32[]{:S(2)}, u32[]{:S(2)}) collective-permute-start(bf16[512,256]{1,0:T(8,128)(2,1)S(1)} %bitcast_multiply_fusion), channel_id=1, source_target_pairs={{0,2},{2,0},{4,6},{6,4},{1,3},{3,1},{5,7},{7,5},{8,10},{10,8},{12,... | collective-permute-start | bytes 786440 | tf_op jit(solution)/shard_map/ppermute | solution.py:11
  66.5 26.6 %collective-permute-start.3 = (bf16[512,512]{1,0:T(8,128)(2,1)S(1)}, bf16[512,512]{1,0:T(8,128)(2,1)S(1)}, u32[]{:S(2)}, u32[]{:S(2)}) collective-permute-start(bf16[512,512]{1,0:T(8,128)(2,1)S(1)} %maximum_select_fusion.5), channel_id=1, source_target_pairs={{0,4},{2,6},{4,0},{6,2},{1,5},{3,7},{5,1},{7,3},{8,12},{10,14},{12... | collective-permute-start | bytes 1572872 | tf_op jit(solution)/shard_map/ppermute | solution.py:11
Sparse Core Ops, SparseCore 0:
  9.5 30.6 all-gather.2
  43.6 19.8 reduce-scatter.2
  65.1 27.9 all-gather.4
  96.6 19.7 reduce-scatter.4
